TPU v7x, 256 devices: a whole 4x4x8 slice. The times are simulated.
256 devices in a mesh: leaf: 8 (over x, core), row: 32 (over y, z).
Axes of the slice: x: 4, y: 4, z: 8, core: 2. Of those that a mesh axis runs over, the one named last changes fastest.
Arguments:
- loc_rhs: float32 [8, 32, 512, 128], P('leaf', 'row'), may hold values from -6 to 6
- loc_inverse: float32 [8, 32, 512, 512], P('leaf', 'row'), may hold values from -0.25 to 0.25
- loc_coupling: float32 [8, 32, 512, 512], P('leaf', 'row'), may hold values from -0.09375 to 0.09375
- loc_pivots: float32 [8, 32, 512], P('leaf', 'row'), may hold values from 0.5 to 4
- pattern: int32 [8, 32, 4], P('leaf', 'row'), may hold values from 0 to 29, as said below
- win_rhs: float32 [4, 2048, 128], P(None, ('leaf', 'row')), may hold values from -6 to 6
- win_pivots: float32 [4, 2048], P(None, ('leaf', 'row')), may hold values from 0.5 to 4
- win_inverse: float32 [32, 120, 2048], P('row', None, 'leaf'), may hold values from -0.125 to 0.125
- win_coupling: float32 [32, 112, 2048], P('row', None, 'leaf'), may hold values from -0.125 to 0.125
Outputs:
- loc_solution: float32 [8, 32, 512, 128], P('leaf', 'row')
- win_solution: float32 [4, 2048, 128], P(None, ('leaf', 'row'))
Inputs may be any that keep to these rules, and one draw needn't show every extreme that they name: `pattern`: on each device the 4 tile numbers are distinct; number p stands for rows p * 128 to (p + 1) * 128 - 1 of the path of the device's leaf index.
All inputs are finite; a program needn't handle non-finite values.
Results may differ from a plain program's by a relative error of at most 0.0001.
Values sent between devices are 32-bit elements; how exact they have to be, the bound alone decides.
A program may use at most 64 MiB of HBM per device.

v0:
```python
import jax
import jax.numpy as jnp
from jax import lax
from jax.sharding import PartitionSpec as P

BASE = 256
TILE = 128
PRECISE = lax.Precision.HIGHEST


def contract_first(left, right):
    return lax.dot_general(left, right, (((0,), (0,)), ((), ())), precision=PRECISE)


def group_sum(partial_value, height, leaf_id, leaf_count):
    group_span = 2**height
    if group_span == 1:
        return partial_value[0]
    padded = jnp.zeros((leaf_count,) + partial_value.shape[1:], jnp.float32)
    padded = lax.dynamic_update_slice_in_dim(
        padded, partial_value, leaf_id // group_span * group_span, 0
    )
    return lax.psum_scatter(padded, "leaf", scatter_dimension=0, tiled=True)[0]


def group_gather(piece, height, leaf_id):
    group_span = 2**height
    if group_span == 1:
        return piece[None]
    whole_set = lax.all_gather(piece[None], "leaf", axis=0, tiled=True)
    return lax.dynamic_slice_in_dim(whole_set, leaf_id // group_span * group_span, group_span, 0)


def masked_block(diag_block, group_span, piece_rows, rank_id, leaf_id):
    row_ids = (
        jnp.arange(group_span)[:, None] * BASE
        + rank_id * piece_rows
        + jnp.arange(piece_rows)[None, :]
    ).reshape(-1)
    col_ids = leaf_id % group_span * BASE + jnp.arange(BASE)
    return jnp.where(col_ids[None, :] < row_ids[:, None], diag_block, 0.0)


def shards(
    loc_rhs,
    loc_inverse,
    loc_coupling,
    loc_pivots,
    pattern,
    win_rhs,
    win_pivots,
    win_inverse,
    win_coupling,
):
    leaf_count = lax.axis_size("leaf")
    rank_count = lax.axis_size("row")
    leaf_id = lax.axis_index("leaf")
    rank_id = lax.axis_index("row")
    levels = win_rhs.shape[0]
    piece_rows = win_rhs.shape[1]
    columns = win_rhs.shape[2]
    groups_total = 2 * leaf_count - 1
    tile_groups = BASE // TILE
    tile_pieces = TILE // piece_rows
    inverse = loc_inverse[0, 0]
    coupling = loc_coupling[0, 0]
    tile_count = coupling.shape[0] // TILE
    own_tiles = pattern[0, 0]
    positions = jnp.arange(inverse.shape[0])
    strict_low = jnp.where(positions[None, :] < positions[:, None], inverse, 0.0)
    solved_loc = loc_rhs[0, 0] + jnp.dot(strict_low, loc_rhs[0, 0], precision=PRECISE)
    loc_terms = jnp.dot(coupling, solved_loc, precision=PRECISE).reshape(
        tile_count, tile_pieces, piece_rows, columns
    )
    slot_ids = jnp.arange(groups_total)[:, None] * tile_groups + jnp.arange(tile_groups)[None, :]
    selector = (slot_ids[:, :, None] == own_tiles[None, None, :]).astype(jnp.float32)
    local_sums = []
    placed = jnp.einsum("ght,tsix->ghsix", selector, loc_terms, precision=PRECISE)
    placed = placed.reshape(groups_total, rank_count, piece_rows, columns)
    padded_levels = []
    for height in range(levels):
        group_span = 2**height
        padded = jnp.zeros((leaf_count, rank_count, piece_rows, columns), jnp.float32)
        segment = placed[group_span - 1 : 2 * group_span - 1]
        padded_levels.append(
            lax.dynamic_update_slice_in_dim(padded, segment, leaf_id // group_span * group_span, 0)
        )
    stacked = jnp.stack(padded_levels).reshape(levels, leaf_count * rank_count, piece_rows, columns)
    summed = lax.psum_scatter(stacked, ("leaf", "row"), scatter_dimension=1, tiled=True)
    for height in range(levels):
        local_sums.append(summed[height, 0])
    from_children = jnp.zeros((piece_rows, columns), jnp.float32)
    solved = []
    diagonals = []
    for height in range(levels):
        group_span = 2**height
        diag_block = win_inverse[
            0, (group_span - 1) * piece_rows : (2 * group_span - 1) * piece_rows
        ]
        strict = masked_block(diag_block, group_span, piece_rows, rank_id, leaf_id)
        diagonals.append(strict)
        residual = win_rhs[height] - local_sums[height] - from_children
        gathered = lax.all_gather(residual, "row", axis=0, tiled=True)
        partial_value = jnp.dot(strict, gathered, precision=PRECISE).reshape(
            group_span, piece_rows, columns
        )
        current = residual + group_sum(partial_value, height, leaf_id, leaf_count)
        solved.append(current)
        if height + 1 < levels:
            spread = lax.all_gather(current, "row", axis=0, tiled=True)
            link_block = win_coupling[
                0, (2 * group_span - 2) * piece_rows : (4 * group_span - 2) * piece_rows
            ]
            coupled = jnp.dot(link_block, spread, precision=PRECISE).reshape(
                2 * group_span, piece_rows, columns
            )
            from_children = group_sum(coupled, height + 1, leaf_id, leaf_count)
    from_parent = jnp.zeros((piece_rows, columns), jnp.float32)
    results = [None] * levels
    spreads = [None] * levels
    for height in reversed(range(levels)):
        group_span = 2**height
        wanted = solved[height] / win_pivots[height][:, None] - from_parent
        rows_in = group_gather(wanted, height, leaf_id)
        partial_value = contract_first(
            diagonals[height], rows_in.reshape(group_span * piece_rows, columns)
        )
        current = wanted + lax.psum_scatter(partial_value, "row", scatter_dimension=0, tiled=True)
        results[height] = current
        spreads[height] = group_gather(current, height, leaf_id)
        if height > 0:
            child_span = group_span // 2
            link_block = win_coupling[
                0, (2 * child_span - 2) * piece_rows : (4 * child_span - 2) * piece_rows
            ]
            partial_value = contract_first(
                link_block, spreads[height].reshape(group_span * piece_rows, columns)
            )
            from_parent = lax.psum_scatter(partial_value, "row", scatter_dimension=0, tiled=True)
    stacked_out = jnp.stack(results)[:, None]
    whole_set = lax.all_gather(stacked_out, ("leaf", "row"), axis=1, tiled=True)
    whole_set = whole_set.reshape(levels, leaf_count, rank_count, piece_rows, columns)
    group_parts = []
    for height in range(levels):
        group_span = 2**height
        group_parts.append(
            lax.dynamic_slice_in_dim(
                whole_set[height], leaf_id // group_span * group_span, group_span, 0
            )
        )
    ordered = jnp.concatenate(group_parts, 0)
    ordered = ordered.reshape(groups_total, tile_groups, tile_pieces, piece_rows, columns)
    picked = jnp.einsum("ght,ghsix->tsix", selector, ordered, precision=PRECISE).reshape(
        tile_count * TILE, columns
    )
    scaled_loc = solved_loc / loc_pivots[0, 0][:, None]
    remainder = scaled_loc - contract_first(coupling, picked)
    answer = remainder + contract_first(strict_low, remainder)
    return (answer[None, None], jnp.stack(results))


def solution(mesh):
    return jax.shard_map(
        shards,
        mesh=mesh,
        in_specs=(
            P("leaf", "row", None, None),
            P("leaf", "row", None, None),
            P("leaf", "row", None, None),
            P("leaf", "row", None),
            P("leaf", "row", None),
            P(None, ("leaf", "row"), None),
            P(None, ("leaf", "row")),
            P("row", None, "leaf"),
            P("row", None, "leaf"),
        ),
        out_specs=(P("leaf", "row", None, None), P(None, ("leaf", "row"), None)),
        check_vma=False,
    )
```

profile of v0, /device:TPU:1, one launch (start us, length us, event | category | flops | bytes accessed | tf_op | source)
XLA Modules:
  0.0 1942.4 jit_solution(597287896424331740)
XLA Ops:
  23.4 271.0 %all-reduce.23.cloned.1.call-done = f32[4,256,8,128]{3,2,1,0:T(8,128)} async-done(((f32[4,256,8,128]{3,2,1,0:T(8,128)}), f32[4,256,8,128]{3,2,1,0:T(8,128)}) %all-reduce.23.cloned.1.call-update) | async-done | bytes 4194320
  295.1 34.5 %all_gather.42 = f32[256,128]{1,0:T(8,128)S(1)} all-gather(f32[8,128]{1,0:T(8,128)S(1)} %fusion.107), channel_id=1, replica_groups=mesh['leaf'=8,'row'=32] {'row'}, dimensions={0}, use_global_device_ids=true | all-gather | bytes 135168 | tf_op jit(solution)/shard_map/all_gather | solution.py:103
  329.8 32.6 %all_gather.43 = f32[256,128]{1,0:T(8,128)S(1)} all-gather(f32[8,128]{1,0:T(8,128)S(1)} %convolution_add_fusion.2), channel_id=1, replica_groups=mesh['leaf'=8,'row'=32] {'row'}, dimensions={0}, use_global_device_ids=true | all-gather | bytes 135168 | tf_op jit(solution)/shard_map/all_gather | solution.py:110
  362.5 38.8 %all-reduce.1 = f32[8,8,128]{2,1,0:T(8,128)S(1)} all-reduce(f32[8,8,128]{2,1,0:T(8,128)S(1)} %fusion.14), channel_id=9, replica_groups=mesh['leaf'=8,'row'=32] {'leaf'}, use_global_device_ids=true, to_apply=%region_1.2.clone | all-reduce | flops 8192 | bytes 65536
  402.7 32.9 %all_gather.44 = f32[256,128]{1,0:T(8,128)S(1)} all-gather(f32[8,128]{1,0:T(8,128)S(1)} %fusion.91), channel_id=1, replica_groups=mesh['leaf'=8,'row'=32] {'row'}, dimensions={0}, use_global_device_ids=true | all-gather | bytes 135168 | tf_op jit(solution)/shard_map/all_gather | solution.py:103
  435.8 33.1 %all-reduce.2 = f32[8,8,128]{2,1,0:T(8,128)S(1)} all-reduce(f32[8,8,128]{2,1,0:T(8,128)S(1)} %convolution_dynamic-update-slice_fusion.1), channel_id=10, replica_groups=mesh['leaf'=8,'row'=32] {'leaf'}, use_global_device_ids=true, to_apply=%region_2.3.clone | all-reduce | flops 8192 | bytes 65536
  469.6 30.8 %all_gather.45 = f32[256,128]{1,0:T(8,128)S(1)} all-gather(f32[8,128]{1,0:T(8,128)S(1)} %fusion.93), channel_id=1, replica_groups=mesh['leaf'=8,'row'=32] {'row'}, dimensions={0}, use_global_device_ids=true | all-gather | bytes 135168 | tf_op jit(solution)/shard_map/all_gather | solution.py:110
  500.6 33.7 %all-reduce.3 = f32[8,8,128]{2,1,0:T(8,128)S(1)} all-reduce(f32[8,8,128]{2,1,0:T(8,128)S(1)} %fusion.13), channel_id=11, replica_groups=mesh['leaf'=8,'row'=32] {'leaf'}, use_global_device_ids=true, to_apply=%region_3.4.clone | all-reduce | flops 8192 | bytes 65536
  535.7 32.2 %all_gather.46 = f32[256,128]{1,0:T(8,128)S(1)} all-gather(f32[8,128]{1,0:T(8,128)S(1)} %fusion.95), channel_id=1, replica_groups=mesh['leaf'=8,'row'=32] {'row'}, dimensions={0}, use_global_device_ids=true | all-gather | bytes 135168 | tf_op jit(solution)/shard_map/all_gather | solution.py:103
  568.2 33.7 %all-reduce.4 = f32[8,8,128]{2,1,0:T(8,128)S(1)} all-reduce(f32[8,8,128]{2,1,0:T(8,128)S(1)} %convolution_dynamic-update-slice_fusion), channel_id=12, replica_groups=mesh['leaf'=8,'row'=32] {'leaf'}, use_global_device_ids=true, to_apply=%region_4.5.clone | all-reduce | flops 8192 | bytes 65536
  602.5 30.8 %all_gather.47 = f32[256,128]{1,0:T(8,128)S(1)} all-gather(f32[8,128]{1,0:T(8,128)S(1)} %fusion.97), channel_id=1, replica_groups=mesh['leaf'=8,'row'=32] {'row'}, dimensions={0}, use_global_device_ids=true | all-gather | bytes 135168 | tf_op jit(solution)/shard_map/all_gather | solution.py:110
  633.6 33.7 %all-reduce.5 = f32[8,8,128]{2,1,0:T(8,128)S(1)} all-reduce(f32[8,8,128]{2,1,0:T(8,128)S(1)} %convolution_bitcast_fusion.5), channel_id=13, replica_groups=mesh['leaf'=8,'row'=32] {'leaf'}, use_global_device_ids=true, to_apply=%region_5.6.clone | all-reduce | flops 8192 | bytes 65536
  668.6 32.2 %all_gather.48 = f32[256,128]{1,0:T(8,128)S(1)} all-gather(f32[8,128]{1,0:T(8,128)S(1)} %bitcast_subtract_fusion.1), channel_id=1, replica_groups=mesh['leaf'=8,'row'=32] {'row'}, dimensions={0}, use_global_device_ids=true | all-gather | bytes 135168 | tf_op jit(solution)/shard_map/all_gather | solution.py:103
  701.1 33.7 %all-reduce.6 = f32[8,8,128]{2,1,0:T(8,128)S(1)} all-reduce(f32[8,8,128]{2,1,0:T(8,128)S(1)} %fusion.25), channel_id=14, replica_groups=mesh['leaf'=8,'row'=32] {'leaf'}, use_global_device_ids=true, to_apply=%region_6.7.clone | all-reduce | flops 8192 | bytes 65536
  755.0 133.2 %all-reduce.25.cloned.1.call-done = f32[256,128]{1,0:T(8,128)} async-done(((f32[256,128]{1,0:T(8,128)}), f32[256,128]{1,0:T(8,128)}) %all-reduce.25.cloned.1.call-update) | async-done | bytes 131088
  889.6 18.0 all-gather
  908.8 135.5 %all-reduce.27.cloned.1.call-done = f32[256,128]{1,0:T(8,128)} async-done(((f32[256,128]{1,0:T(8,128)}), f32[256,128]{1,0:T(8,128)}) %all-reduce.27.cloned.1.call-update) | async-done | bytes 131088
  1045.0 18.0 all-gather.1
  1064.2 135.5 %all-reduce.29.cloned.1.call-done = f32[256,128]{1,0:T(8,128)} async-done(((f32[256,128]{1,0:T(8,128)}), f32[256,128]{1,0:T(8,128)}) %all-reduce.29.cloned.1.call-update) | async-done | bytes 131088
  1219.7 135.5 %all-reduce.31.cloned.1.call-done = f32[256,128]{1,0:T(8,128)} async-done(((f32[256,128]{1,0:T(8,128)}), f32[256,128]{1,0:T(8,128)}) %all-reduce.31.cloned.1.call-update) | async-done | bytes 131088
  1375.1 135.5 %all-reduce.33.cloned.1.call-done = f32[256,128]{1,0:T(8,128)} async-done(((f32[256,128]{1,0:T(8,128)}), f32[256,128]{1,0:T(8,128)}) %all-reduce.33.cloned.1.call-update) | async-done | bytes 131088
  1530.4 135.5 %all-reduce.35.cloned.1.call-done = f32[256,128]{1,0:T(8,128)} async-done(((f32[256,128]{1,0:T(8,128)}), f32[256,128]{1,0:T(8,128)}) %all-reduce.35.cloned.1.call-update) | async-done | bytes 131088
  1667.9 143.1 %all-reduce.37.cloned.1.call-done = f32[256,128]{1,0:T(8,128)} async-done(((f32[256,128]{1,0:T(8,128)}), f32[256,128]{1,0:T(8,128)}) %all-reduce.37.cloned.1.call-update) | async-done | bytes 131088
  1812.3 114.2 %all-gather.8.cloned.1.call-done = f32[4,2048,128]{2,1,0:T(8,128)} async-done(((f32[4,8,128]{2,1,0:T(8,128)}), f32[4,2048,128]{2,1,0:T(8,128)}) %all-gather.8.cloned.1.call-update) | async-done | bytes 4194320 | tf_op jit(solution)/shard_map/all_gather | solution.py:141
  (125 shorter events, 119.7 us)
Async XLA Ops:
  7.2 2.4 copy-start
  7.2 287.2 %all-reduce.23.cloned.1.call-start = ((), (), s32[]{:S(2)}) async-start(), calls=%async_computation.1 | async-start | bytes 8388608
  16.8 2.7 copy-start.2
  21.9 0.7 copy-start.10
  21.9 1.5 copy-start.6
  21.9 272.5 %copy-start.5 = (f32[4,8,128]{2,1,0:T(8,128)S(1)}, f32[4,8,128]{2,1,0:T(8,128)}, u32[]{:S(2)}) copy-start(f32[4,8,128]{2,1,0:T(8,128)} %param.14) | copy-start | bytes 49156
  22.0 307.6 %copy-start.3 = (f32[1,120,256]{2,1,0:T(8,128)S(1)}, f32[1,120,256]{2,1,0:T(8,128)}, u32[]{:S(2)}) copy-start(f32[1,120,256]{2,1,0:T(8,128)} %param.16) | copy-start | bytes 368644
  22.0 340.4 %copy-start.4 = (f32[1,112,256]{2,1,0:T(8,128)S(1)}, f32[1,112,256]{2,1,0:T(8,128)}, u32[]{:S(2)}) copy-start(f32[1,112,256]{2,1,0:T(8,128)} %param.17) | copy-start | bytes 344068
  22.0 731.9 %copy-start.9 = (u32[256]{0:T(256)S(1)}, u32[256]{0:T(256)}, u32[]{:S(2)}) copy-start(u32[256]{0:T(256)} %constant.167) | copy-start | bytes 3076
  22.0 866.2 %all-reduce.25.cloned.1.call-start = ((), (), s32[]{:S(2)}) async-start(), calls=%async_computation.2 | async-start | bytes 262144
  753.6 290.7 %all-reduce.27.cloned.1.call-start = ((), (), s32[]{:S(2)}) async-start(), calls=%async_computation.3 | async-start | bytes 262144
  908.7 291.1 %all-reduce.29.cloned.1.call-start = ((), (), s32[]{:S(2)}) async-start(), calls=%async_computation.4 | async-start | bytes 262144
  1064.2 291.0 %all-reduce.31.cloned.1.call-start = ((), (), s32[]{:S(2)}) async-start(), calls=%async_computation.5 | async-start | bytes 262144
  1219.5 291.1 %all-reduce.33.cloned.1.call-start = ((), (), s32[]{:S(2)}) async-start(), calls=%async_computation.6 | async-start | bytes 262144
  1375.0 291.0 %all-reduce.35.cloned.1.call-start = ((), (), s32[]{:S(2)}) async-start(), calls=%async_computation.7 | async-start | bytes 262144
  1530.4 280.5 %all-reduce.37.cloned.1.call-start = ((), (), s32[]{:S(2)}) async-start(), calls=%async_computation.8 | async-start | bytes 262144
  1667.8 258.7 %all-gather.8.cloned.1.call-start = ((), (), s32[]{:S(2)}) async-start(), calls=%async_computation | async-start | bytes 4210688 | tf_op jit(solution)/shard_map/all_gather | solution.py:141
  1929.0 1.5 copy-start.8
  1929.1 3.0 copy-start.7
  1930.0 3.9 copy-start.1
Sparse Core Ops, SparseCore 0:
  22.1 272.2 all-reduce.22
  753.7 134.3 all-reduce.24
  908.8 135.4 all-reduce.26
  1064.3 135.4 all-reduce.28
  1219.7 135.4 all-reduce.30
  1375.1 135.4 all-reduce.32
  1530.5 135.4 all-reduce.34
  1670.0 140.8 all-reduce.36
  1815.1 111.3 all-gather.7
where the time goes:
time: 1940 us
  waiting for transfers between devices  1340 us (69%)
  blocking collectives  539 us (28%)
    unnamed x17, waiting for transfers between devices  1220 us
    unnamed x6, blocking collectives  207 us
    all_gather x4, blocking collectives, shards(): gathered = lax.all_gather(residual, 'row', axis=0, tiled=True)  132 us
    all_gather x1, waiting for transfers between devices, shards(): whole_set = lax.all_gather(stacked_out, ('leaf', 'row'), axis=1, tiled=True)  114 us
    all_gather x6, blocking collectives, group_gather(): whole_set = lax.all_gather(piece[None], 'leaf', axis=0, tiled=True)  106 us
    all_gather x3, blocking collectives, shards(): spread = lax.all_gather(current, 'row', axis=0, tiled=True)  94.2 us
  transfers between devices with their start and end apart: 9, of which 9 were waited for; matrix products, arithmetic and copies ran while one was open for 0% of the time, Pallas kernels for 0%

commit v1 on v0

--- a/solution.py
+++ b/solution.py
@@ -138,7 +138,10 @@
             )
             from_parent = lax.psum_scatter(partial_value, "row", scatter_dimension=0, tiled=True)
     stacked_out = jnp.stack(results)[:, None]
-    whole_set = lax.all_gather(stacked_out, ("leaf", "row"), axis=1, tiled=True)
+    size = lax.axis_size(("leaf", "row"))
+    blocks = jnp.stack([stacked_out for _ in range(size)])
+    blocks = lax.all_to_all(blocks, ("leaf", "row"), split_axis=0, concat_axis=0)
+    whole_set = jnp.concatenate(blocks, axis=1)
     whole_set = whole_set.reshape(levels, leaf_count, rank_count, piece_rows, columns)
     group_parts = []
     for height in range(levels):

time: 1940 us -> 1940 us (level)
  waiting for transfers between devices: 1340 us -> 1220 us
  blocking collectives: 539 us -> 651 us
    all_gather x1 -> x0, waiting for transfers between devices: 114 us -> none  [shards(): whole_set = lax.all_gather(stacked_out, ('leaf', 'row'), axis=1, tiled=True)]
    all_to_all x0 -> x1, blocking collectives: none -> 112 us  [shards(): lax.all_to_all(blocks, ('leaf', 'row'), split_axis=0, concat_axis=0)]
    unnamed x17 -> x16, waiting for transfers between devices: 1220 us -> 1220 us
  transfers between devices with their start and end apart: 9 -> 8, of which waited for: 9 -> 8; matrix products, arithmetic and copies ran while one was open for 0% -> 0% of each run, Pallas kernels for 0% -> 0%
where the time goes in v1:
time: 1940 us
  waiting for transfers between devices  1220 us (63%)
  blocking collectives  651 us (34%)
    unnamed x16, waiting for transfers between devices  1220 us
    unnamed x6, blocking collectives  207 us
    all_gather x4, blocking collectives, shards(): gathered = lax.all_gather(residual, 'row', axis=0, tiled=True)  132 us
    all_to_all x1, blocking collectives, shards(): lax.all_to_all(blocks, ('leaf', 'row'), split_axis=0, concat_axis=0)  112 us
    all_gather x6, blocking collectives, group_gather(): whole_set = lax.all_gather(piece[None], 'leaf', axis=0, tiled=True)  106 us
    all_gather x3, blocking collectives, shards(): spread = lax.all_gather(current, 'row', axis=0, tiled=True)  94.2 us
  transfers between devices with their start and end apart: 8, of which 8 were waited for; matrix products, arithmetic and copies ran while one was open for 0% of the time, Pallas kernels for 0%

profile of v1, /device:TPU:1, one launch (start us, length us, event | category | flops | bytes accessed | tf_op | source)
XLA Modules:
  0.0 1938.6 jit_solution(16705962793828648094)
XLA Ops:
  23.4 271.0 %all-reduce.23.cloned.1.call-done = f32[4,256,8,128]{3,2,1,0:T(8,128)} async-done(((f32[4,256,8,128]{3,2,1,0:T(8,128)}), f32[4,256,8,128]{3,2,1,0:T(8,128)}) %all-reduce.23.cloned.1.call-update) | async-done | bytes 4194320
  295.1 34.5 %all_gather.39 = f32[256,128]{1,0:T(8,128)S(1)} all-gather(f32[8,128]{1,0:T(8,128)S(1)} %fusion.107), channel_id=1, replica_groups=mesh['leaf'=8,'row'=32] {'row'}, dimensions={0}, use_global_device_ids=true | all-gather | bytes 135168 | tf_op jit(solution)/shard_map/all_gather | solution.py:103
  329.8 32.6 %all_gather.40 = f32[256,128]{1,0:T(8,128)S(1)} all-gather(f32[8,128]{1,0:T(8,128)S(1)} %convolution_add_fusion.2), channel_id=1, replica_groups=mesh['leaf'=8,'row'=32] {'row'}, dimensions={0}, use_global_device_ids=true | all-gather | bytes 135168 | tf_op jit(solution)/shard_map/all_gather | solution.py:110
  362.5 38.8 %all-reduce.1 = f32[8,8,128]{2,1,0:T(8,128)S(1)} all-reduce(f32[8,8,128]{2,1,0:T(8,128)S(1)} %fusion.14), channel_id=8, replica_groups=mesh['leaf'=8,'row'=32] {'leaf'}, use_global_device_ids=true, to_apply=%region_1.2.clone | all-reduce | flops 8192 | bytes 65536
  402.7 32.9 %all_gather.41 = f32[256,128]{1,0:T(8,128)S(1)} all-gather(f32[8,128]{1,0:T(8,128)S(1)} %fusion.91), channel_id=1, replica_groups=mesh['leaf'=8,'row'=32] {'row'}, dimensions={0}, use_global_device_ids=true | all-gather | bytes 135168 | tf_op jit(solution)/shard_map/all_gather | solution.py:103
  435.8 33.1 %all-reduce.2 = f32[8,8,128]{2,1,0:T(8,128)S(1)} all-reduce(f32[8,8,128]{2,1,0:T(8,128)S(1)} %convolution_dynamic-update-slice_fusion.1), channel_id=9, replica_groups=mesh['leaf'=8,'row'=32] {'leaf'}, use_global_device_ids=true, to_apply=%region_2.3.clone | all-reduce | flops 8192 | bytes 65536
  469.6 30.8 %all_gather.42 = f32[256,128]{1,0:T(8,128)S(1)} all-gather(f32[8,128]{1,0:T(8,128)S(1)} %fusion.93), channel_id=1, replica_groups=mesh['leaf'=8,'row'=32] {'row'}, dimensions={0}, use_global_device_ids=true | all-gather | bytes 135168 | tf_op jit(solution)/shard_map/all_gather | solution.py:110
  500.6 33.7 %all-reduce.3 = f32[8,8,128]{2,1,0:T(8,128)S(1)} all-reduce(f32[8,8,128]{2,1,0:T(8,128)S(1)} %fusion.13), channel_id=10, replica_groups=mesh['leaf'=8,'row'=32] {'leaf'}, use_global_device_ids=true, to_apply=%region_3.4.clone | all-reduce | flops 8192 | bytes 65536
  535.7 32.2 %all_gather.43 = f32[256,128]{1,0:T(8,128)S(1)} all-gather(f32[8,128]{1,0:T(8,128)S(1)} %fusion.95), channel_id=1, replica_groups=mesh['leaf'=8,'row'=32] {'row'}, dimensions={0}, use_global_device_ids=true | all-gather | bytes 135168 | tf_op jit(solution)/shard_map/all_gather | solution.py:103
  568.2 33.7 %all-reduce.4 = f32[8,8,128]{2,1,0:T(8,128)S(1)} all-reduce(f32[8,8,128]{2,1,0:T(8,128)S(1)} %convolution_dynamic-update-slice_fusion), channel_id=11, replica_groups=mesh['leaf'=8,'row'=32] {'leaf'}, use_global_device_ids=true, to_apply=%region_4.5.clone | all-reduce | flops 8192 | bytes 65536
  602.5 30.8 %all_gather.44 = f32[256,128]{1,0:T(8,128)S(1)} all-gather(f32[8,128]{1,0:T(8,128)S(1)} %fusion.97), channel_id=1, replica_groups=mesh['leaf'=8,'row'=32] {'row'}, dimensions={0}, use_global_device_ids=true | all-gather | bytes 135168 | tf_op jit(solution)/shard_map/all_gather | solution.py:110
  633.6 33.7 %all-reduce.5 = f32[8,8,128]{2,1,0:T(8,128)S(1)} all-reduce(f32[8,8,128]{2,1,0:T(8,128)S(1)} %convolution_bitcast_fusion.5), channel_id=12, replica_groups=mesh['leaf'=8,'row'=32] {'leaf'}, use_global_device_ids=true, to_apply=%region_5.6.clone | all-reduce | flops 8192 | bytes 65536
  668.6 32.2 %all_gather.45 = f32[256,128]{1,0:T(8,128)S(1)} all-gather(f32[8,128]{1,0:T(8,128)S(1)} %bitcast_subtract_fusion.1), channel_id=1, replica_groups=mesh['leaf'=8,'row'=32] {'row'}, dimensions={0}, use_global_device_ids=true | all-gather | bytes 135168 | tf_op jit(solution)/shard_map/all_gather | solution.py:103
  701.1 33.7 %all-reduce.6 = f32[8,8,128]{2,1,0:T(8,128)S(1)} all-reduce(f32[8,8,128]{2,1,0:T(8,128)S(1)} %fusion.25), channel_id=13, replica_groups=mesh['leaf'=8,'row'=32] {'leaf'}, use_global_device_ids=true, to_apply=%region_6.7.clone | all-reduce | flops 8192 | bytes 65536
  755.0 133.2 %all-reduce.25.cloned.1.call-done = f32[256,128]{1,0:T(8,128)} async-done(((f32[256,128]{1,0:T(8,128)}), f32[256,128]{1,0:T(8,128)}) %all-reduce.25.cloned.1.call-update) | async-done | bytes 131088
  889.6 18.0 all-gather
  908.8 135.5 %all-reduce.27.cloned.1.call-done = f32[256,128]{1,0:T(8,128)} async-done(((f32[256,128]{1,0:T(8,128)}), f32[256,128]{1,0:T(8,128)}) %all-reduce.27.cloned.1.call-update) | async-done | bytes 131088
  1045.0 18.0 all-gather.1
  1064.2 135.5 %all-reduce.29.cloned.1.call-done = f32[256,128]{1,0:T(8,128)} async-done(((f32[256,128]{1,0:T(8,128)}), f32[256,128]{1,0:T(8,128)}) %all-reduce.29.cloned.1.call-update) | async-done | bytes 131088
  1219.7 135.5 %all-reduce.31.cloned.1.call-done = f32[256,128]{1,0:T(8,128)} async-done(((f32[256,128]{1,0:T(8,128)}), f32[256,128]{1,0:T(8,128)}) %all-reduce.31.cloned.1.call-update) | async-done | bytes 131088
  1375.1 135.5 %all-reduce.33.cloned.1.call-done = f32[256,128]{1,0:T(8,128)} async-done(((f32[256,128]{1,0:T(8,128)}), f32[256,128]{1,0:T(8,128)}) %all-reduce.33.cloned.1.call-update) | async-done | bytes 131088
  1530.4 135.5 %all-reduce.35.cloned.1.call-done = f32[256,128]{1,0:T(8,128)} async-done(((f32[256,128]{1,0:T(8,128)}), f32[256,128]{1,0:T(8,128)}) %all-reduce.35.cloned.1.call-update) | async-done | bytes 131088
  1667.8 143.1 %all-reduce.37.cloned.1.call-done = f32[256,128]{1,0:T(8,128)} async-done(((f32[256,128]{1,0:T(8,128)}), f32[256,128]{1,0:T(8,128)}) %all-reduce.37.cloned.1.call-update) | async-done | bytes 131088
  1812.2 112.1 %all_to_all.5 = f32[256,4,1,8,128]{4,3,2,1,0:T(8,128)S(1)} all-to-all(f32[256,4,1,8,128]{4,3,2,1,0:T(8,128)S(1)} %stack.51), channel_id=1, replica_groups=mesh['leaf'=8,'row'=32] {'leaf','row'}, dimensions={0} | all-to-all | bytes 8388608 | tf_op jit(solution)/shard_map/all_to_all | solution.py:143
  (127 shorter events, 117.6 us)
Async XLA Ops:
  7.2 2.4 copy-start
  7.2 287.2 %all-reduce.23.cloned.1.call-start = ((), (), s32[]{:S(2)}) async-start(), calls=%async_computation.1 | async-start | bytes 8388608
  16.8 2.7 copy-start.2
  21.9 0.7 copy-start.11
  21.9 1.5 copy-start.7
  21.9 272.5 %copy-start.6 = (f32[4,8,128]{2,1,0:T(8,128)S(1)}, f32[4,8,128]{2,1,0:T(8,128)}, u32[]{:S(2)}) copy-start(f32[4,8,128]{2,1,0:T(8,128)} %param.14) | copy-start | bytes 49156
  22.0 307.6 %copy-start.3 = (f32[1,120,256]{2,1,0:T(8,128)S(1)}, f32[1,120,256]{2,1,0:T(8,128)}, u32[]{:S(2)}) copy-start(f32[1,120,256]{2,1,0:T(8,128)} %param.16) | copy-start | bytes 368644
  22.0 340.4 %copy-start.4 = (f32[1,112,256]{2,1,0:T(8,128)S(1)}, f32[1,112,256]{2,1,0:T(8,128)}, u32[]{:S(2)}) copy-start(f32[1,112,256]{2,1,0:T(8,128)} %param.17) | copy-start | bytes 344068
  22.0 731.9 %copy-start.10 = (u32[256]{0:T(256)S(1)}, u32[256]{0:T(256)}, u32[]{:S(2)}) copy-start(u32[256]{0:T(256)} %constant.167) | copy-start | bytes 3076
  22.0 866.2 %all-reduce.25.cloned.1.call-start = ((), (), s32[]{:S(2)}) async-start(), calls=%async_computation.2 | async-start | bytes 262144
  753.6 290.7 %all-reduce.27.cloned.1.call-start = ((), (), s32[]{:S(2)}) async-start(), calls=%async_computation.3 | async-start | bytes 262144
  908.7 291.1 %all-reduce.29.cloned.1.call-start = ((), (), s32[]{:S(2)}) async-start(), calls=%async_computation.4 | async-start | bytes 262144
  1064.2 291.0 %all-reduce.31.cloned.1.call-start = ((), (), s32[]{:S(2)}) async-start(), calls=%async_computation.5 | async-start | bytes 262144
  1219.5 291.1 %all-reduce.33.cloned.1.call-start = ((), (), s32[]{:S(2)}) async-start(), calls=%async_computation.6 | async-start | bytes 262144
  1375.0 291.0 %all-reduce.35.cloned.1.call-start = ((), (), s32[]{:S(2)}) async-start(), calls=%async_computation.7 | async-start | bytes 262144
  1530.4 280.5 %all-reduce.37.cloned.1.call-start = ((), (), s32[]{:S(2)}) async-start(), calls=%async_computation.8 | async-start | bytes 262144
  1811.7 112.7 %copy-start.5 = (f32[4,8,128]{2,1,0:T(8,128)}, f32[4,8,128]{2,1,0:T(8,128)S(1)}, u32[]{:S(2)}) copy-start(f32[4,8,128]{2,1,0:T(8,128)S(1)} %pad_maximum_fusion.1) | copy-start | bytes 49156
  1924.9 1.5 copy-start.9
  1925.0 3.0 copy-start.8
  1925.9 3.9 copy-start.1
Sparse Core Ops, SparseCore 0:
  22.1 272.2 all-reduce.22
  753.7 134.3 all-reduce.24
  908.8 135.4 all-reduce.26
  1064.3 135.4 all-reduce.28
  1219.7 135.4 all-reduce.30
  1375.1 135.4 all-reduce.32
  1530.5 135.4 all-reduce.34
  1670.0 140.8 all-reduce.36
